TPU v7x, 32 devices: a whole 2x2x4 slice. The times are simulated.
32 devices in a mesh: crop: 1, res: 32 (over z, y, x, core).
Axes of the slice: x: 2, y: 2, z: 4, core: 2. Of those that a mesh axis runs over, the one named last changes fastest.
Arguments:
- homolog_symbol_ids: int32 [64, 128], P(('crop', 'res')), may hold values from 0 to 22
- residue_attend_mask: int32 [128], P('crop'), may hold values 0 or 1
- alignment_state: bfloat16 [64, 128, 256], P(('crop', 'res')), may hold values from -6 to 6
- pair: bfloat16 [128, 128, 128], P(('crop', 'res')), may hold values from -6 to 6
- symbol_lookup_matrix: bfloat16 [23, 256], replicated, may hold values from -3 to 3
- pair_bias_weight: bfloat16 [128, 8], replicated, may hold values from -0.5 to 0.5
- row_projection_weight: bfloat16 [256, 1024], replicated, may hold values from -8 to 8
- horizontal_readout_matrix: bfloat16 [256, 256], replicated, may hold values from -0.375 to 0.375
- column_projection_weight: bfloat16 [256, 1024], replicated, may hold values from -8 to 8
- vertical_readout_matrix: bfloat16 [256, 256], replicated, may hold values from -0.375 to 0.375
- product_factor_matrices: bfloat16 [256, 64], replicated, may hold values from -0.375 to 0.375
- outer_output_weight: bfloat16 [1024, 128], replicated, may hold values from -1.5 to 1.5
- triangle_input_weight: bfloat16 [128, 640], replicated, may hold values from -0.5 to 0.5
- triangle_output_weight: bfloat16 [128, 128], replicated, may hold values from -0.5 to 0.5
Outputs:
- alignment_output: bfloat16 [64, 128, 256], P('crop', 'res')
- pair_output: bfloat16 [128, 128, 128], P(('crop', 'res'))
All inputs are finite; a program needn't handle non-finite values.
Results may differ from a plain program's by a relative error of at most 0.013.
Values may be sent and summed in bfloat16 or wider, within the bound.
A program may use at most 64 MiB of HBM per device.

v0:
```python
import jax
import jax.numpy as jnp
from jax import lax
from jax.sharding import PartitionSpec as P

EPSILON = 1e-05


def layer_normalized(input_rows, axis):
    average = jnp.mean(input_rows, axis, keepdims=True)
    centred = input_rows - average
    spread = jnp.mean(centred * centred, axis, keepdims=True)
    return centred * lax.rsqrt(spread + EPSILON)


def split_proj(input_rows, weight, head_count):
    channels = weight.shape[0]
    head_size = channels // head_count
    projected = jnp.einsum("blc,ce->ble", input_rows, weight, preferred_element_type=jnp.float32)
    lead = projected.shape[:2]
    query_tensor = (
        (projected[..., :channels] * head_size ** (-0.5))
        .astype(jnp.bfloat16)
        .reshape(lead + (head_count, head_size))
    )
    key_tensor = (
        projected[..., channels : 2 * channels]
        .astype(jnp.bfloat16)
        .reshape(lead + (head_count, head_size))
    )
    value_tensor = (
        projected[..., 2 * channels : 3 * channels]
        .astype(jnp.bfloat16)
        .reshape(lead + (head_count, head_size))
    )
    gate_values = projected[..., 3 * channels :]
    return (query_tensor, key_tensor, value_tensor, gate_values)


def attention_block_fn(query_tensor, key_tensor, value_tensor, gate_values, extra_bias, out_weight):
    scores = (
        jnp.einsum("bqhd,bkhd->bhqk", query_tensor, key_tensor, preferred_element_type=jnp.float32)
        + extra_bias
    )
    row_top = jnp.max(scores, -1, keepdims=True)
    exp_scores = jnp.exp(scores - row_top)
    weights = (exp_scores / jnp.sum(exp_scores, -1, keepdims=True)).astype(jnp.bfloat16)
    mixed = jnp.einsum("bhqk,bkhd->bqhd", weights, value_tensor, preferred_element_type=jnp.float32)
    gated = (jax.nn.sigmoid(gate_values) * mixed.reshape(gate_values.shape)).astype(jnp.bfloat16)
    return jnp.einsum("bqc,ce->bqe", gated, out_weight, preferred_element_type=jnp.float32)


def shards(
    homolog_symbol_ids,
    residue_attend_mask,
    alignment_state,
    pair,
    symbol_lookup_matrix,
    pair_bias_weight,
    row_projection_weight,
    horizontal_readout_matrix,
    column_projection_weight,
    vertical_readout_matrix,
    product_factor_matrices,
    outer_output_weight,
    triangle_input_weight,
    triangle_output_weight,
):
    residue_count = lax.axis_size("res")
    sequence_total = alignment_state.shape[0] * residue_count
    res_local = pair.shape[0]
    chain_total = pair.shape[1]
    pair_chan = pair.shape[2]
    owner_chan = pair_chan // residue_count
    outer_chan = product_factor_matrices.shape[1] // 2
    head_count = pair_bias_weight.shape[1]
    token_class_count = symbol_lookup_matrix.shape[0]
    one_hot_tokens = (
        homolog_symbol_ids[:, :, None]
        == jnp.arange(token_class_count, dtype=jnp.int32)[None, None, :]
    ).astype(jnp.bfloat16)
    alignment_initial = alignment_state.astype(jnp.float32) + jnp.einsum(
        "kly,yb->klb", one_hot_tokens, symbol_lookup_matrix, preferred_element_type=jnp.float32
    )
    pair_normed = layer_normalized(pair.astype(jnp.float32), -1).astype(jnp.bfloat16)
    bias_local = jnp.einsum(
        "ijc,ch->hij", pair_normed, pair_bias_weight, preferred_element_type=jnp.float32
    ).astype(jnp.bfloat16)
    mask_bias = (residue_attend_mask.astype(jnp.float32) - 1.0) * 10000.0
    row_input = layer_normalized(alignment_initial, -1).astype(jnp.bfloat16)
    query_tensor, key_tensor, value_tensor, gate_values = split_proj(
        row_input, row_projection_weight, head_count
    )
    bias_all = lax.all_gather(bias_local, "res", axis=1, tiled=True)
    extra_bias = bias_all.astype(jnp.float32)[None] + mask_bias[None, None, None, :]
    row_attention_update = attention_block_fn(
        query_tensor, key_tensor, value_tensor, gate_values, extra_bias, horizontal_readout_matrix
    )
    alignment_after_rows = (alignment_initial + row_attention_update).astype(jnp.bfloat16)
    alignment_columns = lax.all_to_all(
        alignment_after_rows, "res", split_axis=1, concat_axis=0, tiled=True
    )
    column_start = jnp.swapaxes(alignment_columns, 0, 1).astype(jnp.float32)
    col_in = layer_normalized(column_start, -1).astype(jnp.bfloat16)
    col_queries, col_keys, col_values, col_gating = split_proj(
        col_in, column_projection_weight, head_count
    )
    alignment_after_columns = column_start + attention_block_fn(
        col_queries, col_keys, col_values, col_gating, jnp.float32(0.0), vertical_readout_matrix
    )
    alignment_output = jnp.swapaxes(alignment_after_columns, 0, 1).astype(jnp.bfloat16)
    outer_input = layer_normalized(alignment_after_columns, -1).astype(jnp.bfloat16)
    factor_ab = jnp.einsum(
        "rsc,ce->rse", outer_input, product_factor_matrices, preferred_element_type=jnp.float32
    )
    left = factor_ab[..., :outer_chan].astype(jnp.bfloat16)
    latter_factor = (
        factor_ab[..., outer_chan:]
        .astype(jnp.bfloat16)
        .reshape(res_local, sequence_total * outer_chan)
    )
    piece = lax.all_gather(latter_factor, "res", axis=0, tiled=True)
    count = piece.shape[0]
    right_rows = piece.reshape(count, sequence_total, outer_chan)
    cross_product_result = (
        jnp.einsum("isc,jsd->ijcd", left, right_rows, preferred_element_type=jnp.float32)
        / sequence_total
    ).astype(jnp.bfloat16)
    update = jnp.einsum(
        "ije,ez->ijz",
        cross_product_result.reshape(res_local, count, outer_chan * outer_chan),
        outer_output_weight,
        preferred_element_type=jnp.float32,
    )
    pair_one = pair.astype(jnp.float32) + update
    tri_normed = layer_normalized(pair_one, -1).astype(jnp.bfloat16)
    factors = jnp.einsum(
        "ijc,ce->eij",
        tri_normed,
        triangle_input_weight[:, : 4 * pair_chan],
        preferred_element_type=jnp.float32,
    )
    gate_out = jnp.einsum(
        "ijc,ce->ije",
        tri_normed,
        triangle_input_weight[:, 4 * pair_chan :],
        preferred_element_type=jnp.float32,
    )
    left_f = (jax.nn.sigmoid(factors[pair_chan : 2 * pair_chan]) * factors[:pair_chan]).astype(
        jnp.bfloat16
    )
    right_f = (
        jax.nn.sigmoid(factors[3 * pair_chan :]) * factors[2 * pair_chan : 3 * pair_chan]
    ).astype(jnp.bfloat16)
    left_f = left_f.reshape(residue_count, owner_chan, res_local, chain_total)
    right_f = right_f.reshape(residue_count, owner_chan, res_local, chain_total)
    combined = jnp.einsum(
        "xcik,xcjk->xcij",
        lax.all_to_all(left_f, "res", split_axis=0, concat_axis=2, tiled=True),
        lax.all_to_all(right_f, "res", split_axis=0, concat_axis=2, tiled=True),
        preferred_element_type=jnp.float32,
    ).astype(jnp.bfloat16)
    back_rows = lax.all_to_all(combined, "res", split_axis=2, concat_axis=0, tiled=True)
    back_rows = back_rows.reshape(pair_chan, res_local, chain_total)
    comb_normed = layer_normalized(back_rows.astype(jnp.float32), 0).astype(jnp.bfloat16)
    tri_update = jnp.einsum(
        "cij,cz->ijz", comb_normed, triangle_output_weight, preferred_element_type=jnp.float32
    )
    pair_output = (pair_one + jax.nn.sigmoid(gate_out) * tri_update).astype(jnp.bfloat16)
    return (alignment_output, pair_output)


def solution(mesh):
    placed = (
        P(("crop", "res"), None),
        P("crop"),
        P(("crop", "res"), None, None),
        P(("crop", "res"), None, None),
        P(),
        P(),
        P(),
        P(),
        P(),
        P(),
        P(),
        P(),
        P(),
        P(),
    )
    return jax.shard_map(
        shards,
        mesh=mesh,
        in_specs=placed,
        out_specs=(P("crop", "res", None), P(("crop", "res"), None, None)),
        check_vma=False,
    )
```

profile of v0, /device:TPU:0, one launch (start us, length us, event | category | flops | bytes accessed | tf_op | source)
XLA Modules:
  0.0 155.3 jit_solution(11216174859262117624)
XLA Ops:
  0.7 0.7 add_multiply_fusion
  1.4 1.0 copy.74
  2.5 0.8 fusion.14
  3.4 43.9 %all_gather.6 = bf16[8,128,128]{2,0,1:T(8,128)(2,1)S(1)} all-gather(bf16[8,4,128]{2,0,1:T(8,128)(2,1)S(1)} %fusion.14), channel_id=1, replica_groups=mesh['crop'=1,'res'=32] {'res'}, dimensions={1}, use_global_device_ids=true | all-gather | bytes 270336 | tf_op jit(solution)/shard_map/all_gather | solution.py:94
  47.3 0.2 copy.76
  47.6 0.3 fusion.84
  48.1 0.3 fusion.85
  48.5 0.7 fusion.83
  49.5 0.5 copy-done.1
  50.1 0.5 fusion.86
  50.6 1.3 convolution_add_fusion
  51.9 1.0 copy.71
  53.0 1.0 fusion.20
  54.0 1.1 copy.78
  55.2 1.1 fusion.11
  56.4 9.9 %all_to_all.48 = bf16[2,128,256]{2,0,1:T(2,128)(2,1)S(1)} all-to-all(bf16[2,128,256]{2,0,1:T(2,128)(2,1)S(1)} %copy.79), channel_id=1, replica_groups=mesh['crop'=1,'res'=32] {'res'}, dimensions={1} | all-to-all | bytes 262144 | tf_op jit(solution)/shard_map/all_to_all | solution.py:100
  66.7 0.2 multiply_reduce_fusion.2
  66.9 0.3 fusion.87
  67.3 0.7 fusion.82
  68.4 0.5 fusion.88
  68.9 0.3 fusion.90
  69.2 1.1 copy.81
  70.3 1.2 fusion.19
  71.4 1.2 copy.85
  72.7 1.1 fusion.46
  73.9 0.2 multiply_reduce_fusion.1
  74.1 0.3 convolution_convert_fusion.1
  74.7 39.3 %all-gather = bf16[32,4,2048]{2,1,0:T(4,128)(2,1)S(1)} all-gather(bf16[1,4,2048]{2,1,0:T(4,128)(2,1)S(1)} %reshape.173), channel_id=1, replica_groups=mesh['crop'=1,'res'=32] {'res'}, dimensions={0}, use_global_device_ids=true | all-gather | bytes 540672 | tf_op jit(solution)/shard_map/all_gather | solution.py:122
  114.0 1.2 reshape.160
  115.2 2.6 %copy.109 = bf16[128,64,32,1]{0,1,3,2:T(8,128)(2,1)S(1)} copy(bf16[128,64,32,1]{2,1,0,3:T(8,128)(2,1)S(1)} %bitcast.133) | data formatting | bytes 1048576 | tf_op jit(solution)/shard_map/reshape | solution.py:124
  117.8 0.4 fusion.6
  118.2 0.7 copy.88
  118.9 0.4 fusion.89
  119.4 0.3 convolution_bitcast_fusion
  120.0 0.7 copy.98
  120.7 2.6 %all-to-all-start.2 = ((bf16[32,4,4,128]{3,1,2,0:T(4,128)(2,1)}), bf16[32,4,4,128]{3,1,2,0:T(4,128)(2,1)S(1)}, u32[]{:S(2)}, u32[]{:S(2)}) async-start(bf16[32,4,4,128]{3,1,2,0:T(4,128)(2,1)} %copy.98), calls=%async_computation.2 | async-start | bytes 262144 | tf_op jit(solution)/shard_map/all_to_all | solution.py:160
  123.4 0.7 copy.95
  124.1 7.4 %all-to-all-done.2 = bf16[32,4,4,128]{3,1,2,0:T(4,128)(2,1)S(1)} async-done(((bf16[32,4,4,128]{3,1,2,0:T(4,128)(2,1)}), bf16[32,4,4,128]{3,1,2,0:T(4,128)(2,1)S(1)}, u32[]{:S(2)}, u32[]{:S(2)}) %all-to-all-start.2) | async-done | bytes 131104 | tf_op jit(solution)/shard_map/all_to_all | solution.py:160
  131.5 2.6 %all-to-all-start.1 = ((bf16[32,4,4,128]{3,1,2,0:T(4,128)(2,1)}), bf16[32,4,4,128]{3,1,2,0:T(4,128)(2,1)S(1)}, u32[]{:S(2)}, u32[]{:S(2)}) async-start(bf16[32,4,4,128]{3,1,2,0:T(4,128)(2,1)} %copy.95), calls=%async_computation.1 | async-start | bytes 262144 | tf_op jit(solution)/shard_map/all_to_all | solution.py:159
  134.1 8.1 %all-to-all-done.1 = bf16[32,4,4,128]{3,1,2,0:T(4,128)(2,1)S(1)} async-done(((bf16[32,4,4,128]{3,1,2,0:T(4,128)(2,1)}), bf16[32,4,4,128]{3,1,2,0:T(4,128)(2,1)S(1)}, u32[]{:S(2)}, u32[]{:S(2)}) %all-to-all-start.1) | async-done | bytes 131104 | tf_op jit(solution)/shard_map/all_to_all | solution.py:159
  142.3 0.2 fusion.13
  142.5 0.8 copy.100
  143.3 2.6 %all-to-all-start.3 = ((bf16[1,4,128,128]{3,1,0,2:T(4,128)(2,1)}), bf16[1,4,128,128]{3,1,0,2:T(4,128)(2,1)S(1)}, u32[]{:S(2)}, u32[]{:S(2)}) async-start(bf16[1,4,128,128]{3,1,0,2:T(4,128)(2,1)} %copy.100), calls=%async_computation.3 | async-start | bytes 262144 | tf_op jit(solution)/shard_map/all_to_all | solution.py:163
  145.9 0.8 copy.104
  146.6 0.3 fusion.10
  146.9 7.2 %all-to-all-done.3 = bf16[1,4,128,128]{3,1,0,2:T(4,128)(2,1)S(1)} async-done(((bf16[1,4,128,128]{3,1,0,2:T(4,128)(2,1)}), bf16[1,4,128,128]{3,1,0,2:T(4,128)(2,1)S(1)}, u32[]{:S(2)}, u32[]{:S(2)}) %all-to-all-start.3) | async-done | bytes 131104 | tf_op jit(solution)/shard_map/all_to_all | solution.py:163
  154.3 0.2 fusion.12
  154.6 0.8 copy.105
  (60 shorter events, 2.9 us)
Async XLA Ops:
  0.6 47.5 %copy-start = (bf16[256,1024]{1,0:T(8,128)(2,1)S(1)}, bf16[256,1024]{1,0:T(8,128)(2,1)}, u32[]{:S(2)}) copy-start(bf16[256,1024]{1,0:T(8,128)(2,1)} %param.20) | copy-start | bytes 1572868
  0.6 46.9 %copy-start.9 = (bf16[23,256]{1,0:T(8,128)(2,1)S(1)}, bf16[23,256]{1,0:T(8,128)(2,1)}, u32[]{:S(2)}) copy-start(bf16[23,256]{1,0:T(8,128)(2,1)} %param.18) | copy-start | bytes 35332
  0.7 46.9 %copy-start.5 = (bf16[2,128,256]{2,1,0:T(8,128)(2,1)S(1)}, bf16[2,128,256]{2,1,0:T(8,128)(2,1)}, u32[]{:S(2)}) copy-start(bf16[2,128,256]{2,1,0:T(8,128)(2,1)} %param.16) | copy-start | bytes 393220
  0.7 46.9 %copy-start.10 = (s32[2,128]{1,0:T(2,128)S(1)}, s32[2,128]{1,0:T(2,128)}, u32[]{:S(2)}) copy-start(s32[2,128]{1,0:T(2,128)} %param.14) | copy-start | bytes 3076
  49.3 0.6 copy-start.1
  49.5 0.7 copy-start.2
  54.0 12.9 %copy-start.3 = (bf16[256,1024]{1,0:T(8,128)(2,1)S(1)}, bf16[256,1024]{1,0:T(8,128)(2,1)}, u32[]{:S(2)}) copy-start(bf16[256,1024]{1,0:T(8,128)(2,1)} %param.22) | copy-start | bytes 1572868
  71.4 2.7 %copy-start.7 = (bf16[256,64]{0,1:T(8,128)(2,1)S(1)}, bf16[256,64]{0,1:T(8,128)(2,1)}, u32[]{:S(2)}) copy-start(bf16[256,64]{0,1:T(8,128)(2,1)} %param.24) | copy-start | bytes 98308
  117.8 1.1 copy-start.4
  118.2 1.1 copy-start.6
  120.7 10.8 %all-to-all-start.2 = ((bf16[32,4,4,128]{3,1,2,0:T(4,128)(2,1)}), bf16[32,4,4,128]{3,1,2,0:T(4,128)(2,1)S(1)}, u32[]{:S(2)}, u32[]{:S(2)}) async-start(bf16[32,4,4,128]{3,1,2,0:T(4,128)(2,1)} %copy.98), calls=%async_computation.2 | async-start | bytes 262144 | tf_op jit(solution)/shard_map/all_to_all | solution.py:160
  123.4 30.9 %copy-start.8 = (bf16[128,128]{1,0:T(8,128)(2,1)S(1)}, bf16[128,128]{1,0:T(8,128)(2,1)}, u32[]{:S(2)}) copy-start(bf16[128,128]{1,0:T(8,128)(2,1)} %param.27) | copy-start | bytes 98308
  131.5 10.8 %all-to-all-start.1 = ((bf16[32,4,4,128]{3,1,2,0:T(4,128)(2,1)}), bf16[32,4,4,128]{3,1,2,0:T(4,128)(2,1)S(1)}, u32[]{:S(2)}, u32[]{:S(2)}) async-start(bf16[32,4,4,128]{3,1,2,0:T(4,128)(2,1)} %copy.95), calls=%async_computation.1 | async-start | bytes 262144 | tf_op jit(solution)/shard_map/all_to_all | solution.py:159
  143.3 10.8 %all-to-all-start.3 = ((bf16[1,4,128,128]{3,1,0,2:T(4,128)(2,1)}), bf16[1,4,128,128]{3,1,0,2:T(4,128)(2,1)S(1)}, u32[]{:S(2)}, u32[]{:S(2)}) async-start(bf16[1,4,128,128]{3,1,0,2:T(4,128)(2,1)} %copy.100), calls=%async_computation.3 | async-start | bytes 262144 | tf_op jit(solution)/shard_map/all_to_all | solution.py:163
where the time goes:
time: 156 us; the launch traced here: 155 us
  blocking collectives  93.2 us (60%)
  waiting for transfers between devices  22.7 us (15%)
  local copies, waits for them, and re-layouts  17.4 us (11%)
  matrix products  11 us (7%)
  starting transfers between devices  7.73 us (5%)
  other arithmetic  2.2 us (1%)
    all_gather x1, blocking collectives, shards(): bias_all = lax.all_gather(bias_local, 'res', axis=1, tiled=True)  43.9 us
    all_gather x1, blocking collectives, shards(): piece = lax.all_gather(latter_factor, 'res', axis=0, tiled=True)  39.3 us
    all_to_all x1, blocking collectives, shards(): lax.all_to_all(alignment_after_rows, 'res', split_axis=1, concat_axis=0,...  9.91 us
    all_to_all x1, waiting for transfers between devices, shards(): lax.all_to_all(left_f, 'res', split_axis=0, concat_axis=2, tiled=True)  8.14 us
    all_to_all x1, waiting for transfers between devices, shards(): lax.all_to_all(right_f, 'res', split_axis=0, concat_axis=2, tiled=True)  7.35 us
    all_to_all x1, waiting for transfers between devices, shards(): lax.all_to_all(combined, 'res', split_axis=2, concat_axis=0, tiled=True)  7.17 us
    reshape x2, local copies, waits for them, and re-layouts, shards(): right_rows = piece.reshape(count, sequence_total, outer_chan)  3.78 us
    unnamed x26, local copies, waits for them, and re-layouts  3.38 us
  transfers between devices with their start and end apart: 3, of which 3 were waited for; matrix products, arithmetic and copies ran while one was open for 1% of the time, Pallas kernels for 0%

commit v1 on v0

--- a/solution.py
+++ b/solution.py
@@ -1,9 +1,62 @@
+import functools
+
 import jax
 import jax.numpy as jnp
 from jax import lax
+from jax.experimental import pallas as pl
+from jax.experimental.pallas import tpu as pltpu
 from jax.sharding import PartitionSpec as P
 
 EPSILON = 1e-05
+MESH = pl.DeviceIdType.MESH
+
+
+def exchange_kernel(count, gather, source, landing, send_sem, recv_sem):
+    me = lax.axis_index("res")
+    barrier = pltpu.get_barrier_semaphore()
+
+    @pl.loop(1, count)
+    def _(step):
+        pl.semaphore_signal(
+            barrier,
+            inc=1,
+            device_id={"res": lax.rem(me + step, count)},
+            device_id_type=MESH,
+        )
+
+    landing[me] = source[...] if gather else source[me]
+    pl.semaphore_wait(barrier, count - 1)
+
+    @pl.loop(1, count)
+    def _(step):
+        peer = lax.rem(me + step, count)
+        pltpu.make_async_remote_copy(
+            src_ref=source if gather else source.at[peer],
+            dst_ref=landing.at[me],
+            send_sem=send_sem,
+            recv_sem=recv_sem,
+            device_id={"res": peer},
+            device_id_type=MESH,
+        ).start()
+
+    others = landing.at[pl.ds(0, count - 1)]
+    pltpu.make_async_copy(others, others, recv_sem).wait()
+    pltpu.make_async_copy(others, others, send_sem).wait()
+
+
+def exchange(operand, gather, number):
+    count = lax.axis_size("res")
+    extent = operand.shape if gather else operand.shape[1:]
+    return pl.pallas_call(
+        functools.partial(exchange_kernel, count, gather),
+        out_shape=jax.ShapeDtypeStruct((count,) + extent, operand.dtype),
+        in_specs=[pl.BlockSpec(memory_space=pltpu.VMEM)],
+        out_specs=pl.BlockSpec(memory_space=pltpu.VMEM),
+        scratch_shapes=[pltpu.SemaphoreType.DMA, pltpu.SemaphoreType.DMA],
+        compiler_params=pltpu.CompilerParams(
+            collective_id=number, has_side_effects=True
+        ),
+    )(operand)
 
 
 def layer_normalized(input_rows, axis):
@@ -91,15 +144,22 @@
     query_tensor, key_tensor, value_tensor, gate_values = split_proj(
         row_input, row_projection_weight, head_count
     )
-    bias_all = lax.all_gather(bias_local, "res", axis=1, tiled=True)
+    bias_all = exchange(bias_local.reshape(-1, chain_total), True, 0)
+    bias_all = jnp.swapaxes(
+        bias_all.reshape(residue_count, head_count, res_local, chain_total), 0, 1
+    ).reshape(head_count, chain_total, chain_total)
     extra_bias = bias_all.astype(jnp.float32)[None] + mask_bias[None, None, None, :]
     row_attention_update = attention_block_fn(
         query_tensor, key_tensor, value_tensor, gate_values, extra_bias, horizontal_readout_matrix
     )
     alignment_after_rows = (alignment_initial + row_attention_update).astype(jnp.bfloat16)
-    alignment_columns = lax.all_to_all(
-        alignment_after_rows, "res", split_axis=1, concat_axis=0, tiled=True
-    )
+    seqs_local, channels = alignment_state.shape[0], alignment_state.shape[2]
+    outgoing = jnp.swapaxes(
+        alignment_after_rows.reshape(seqs_local, residue_count, res_local, channels), 0, 1
+    )
+    alignment_columns = exchange(
+        outgoing.reshape(residue_count, -1, 2 * channels), False, 1
+    ).reshape(sequence_total, res_local, channels)
     column_start = jnp.swapaxes(alignment_columns, 0, 1).astype(jnp.float32)
     col_in = layer_normalized(column_start, -1).astype(jnp.bfloat16)
     col_queries, col_keys, col_values, col_gating = split_proj(
@@ -119,8 +179,8 @@
         .astype(jnp.bfloat16)
         .reshape(res_local, sequence_total * outer_chan)
     )
-    piece = lax.all_gather(latter_factor, "res", axis=0, tiled=True)
-    count = piece.shape[0]
+    piece = exchange(latter_factor.reshape(-1, 128), True, 2)
+    count = chain_total
     right_rows = piece.reshape(count, sequence_total, outer_chan)
     cross_product_result = (
         jnp.einsum("isc,jsd->ijcd", left, right_rows, preferred_element_type=jnp.float32)
@@ -154,13 +214,19 @@
     ).astype(jnp.bfloat16)
     left_f = left_f.reshape(residue_count, owner_chan, res_local, chain_total)
     right_f = right_f.reshape(residue_count, owner_chan, res_local, chain_total)
+    both = jnp.concatenate([left_f, right_f], axis=1)
+    both = exchange(both.reshape(residue_count, -1, chain_total), False, 3)
+    both = both.reshape(residue_count, 2, owner_chan, res_local, chain_total)
+    both = jnp.transpose(both, (1, 2, 0, 3, 4)).reshape(
+        2, owner_chan, chain_total, chain_total
+    )
     combined = jnp.einsum(
-        "xcik,xcjk->xcij",
-        lax.all_to_all(left_f, "res", split_axis=0, concat_axis=2, tiled=True),
-        lax.all_to_all(right_f, "res", split_axis=0, concat_axis=2, tiled=True),
-        preferred_element_type=jnp.float32,
-    ).astype(jnp.bfloat16)
-    back_rows = lax.all_to_all(combined, "res", split_axis=2, concat_axis=0, tiled=True)
+        "cik,cjk->cij", both[0], both[1], preferred_element_type=jnp.float32
+    ).astype(jnp.bfloat16)
+    combined = jnp.swapaxes(
+        combined.reshape(owner_chan, residue_count, res_local, chain_total), 0, 1
+    )
+    back_rows = exchange(combined.reshape(residue_count, -1, chain_total), False, 4)
     back_rows = back_rows.reshape(pair_chan, res_local, chain_total)
     comb_normed = layer_normalized(back_rows.astype(jnp.float32), 0).astype(jnp.bfloat16)
     tri_update = jnp.einsum(

time: 156 us -> 103 us (0.66)
  blocking collectives: 93.2 us -> 0 us
  Pallas kernels: 0 us -> 65.4 us
  waiting for transfers between devices: 22.7 us -> 0 us
  starting transfers between devices: 7.73 us -> 0 us
  local copies, waits for them, and re-layouts: 17.4 us -> 20.9 us
    all_gather x2 -> x0, blocking collectives: 83.3 us -> none  [the longest x1 43.9 us: shards(): bias_all = lax.all_gather(bias_local, 'res', axis=1, tiled=True)]
    pallas_call x0 -> x5, Pallas kernels: none -> 65.4 us  [exchange(): pl.pallas_call(functools.partial(exchange_kernel, count, gather), out_sha...]
    all_to_all x3 -> x0, waiting for transfers between devices: 22.7 us -> none  [the longest x1 8.14 us: shards(): lax.all_to_all(left_f, 'res', split_axis=0, concat_axis=2, tiled=True)]
    all_to_all x1 -> x0, blocking collectives: 9.91 us -> none  [shards(): lax.all_to_all(alignment_after_rows, 'res', split_axis=1, concat_axis=0,...]
    all_to_all x3 -> x0, starting transfers between devices: 7.73 us -> none  [the longest x1 2.58 us: shards(): lax.all_to_all(left_f, 'res', split_axis=0, concat_axis=2, tiled=True)]
    reshape x2, local copies, waits for them, and re-layouts: 2.36 us -> 0.31 us  [attention_block_fn(): mixed.reshape(gate_values.shape)]
    unnamed x26 -> x29, local copies, waits for them, and re-layouts: 3.38 us -> 3.88 us
  transfers between devices with their start and end apart: 3 -> 0, of which waited for: 3 -> 0; matrix products, arithmetic and copies ran while one was open for 1% -> 0% of each run, Pallas kernels for 0% -> 0%
where the time goes in v1:
time: 103 us; the launch traced here: 102 us
  Pallas kernels  65.4 us (63%)
  local copies, waits for them, and re-layouts  20.9 us (20%)
  matrix products  11.5 us (11%)
  other arithmetic  3.39 us (3%)
  between operations  1.21 us (1%)
    pallas_call x5, Pallas kernels, exchange(): pl.pallas_call(functools.partial(exchange_kernel, count, gather), out_sha...  65.4 us
    reshape x2, local copies, waits for them, and re-layouts, shards(): right_rows = piece.reshape(count, sequence_total, outer_chan)  5.29 us
    unnamed x29, local copies, waits for them, and re-layouts  3.88 us
    dot_general x2, matrix products, attention_block_fn(): jnp.einsum('bhqk,bkhd->bqhd', weights, value_tensor, preferred_element_ty...  2.55 us
    dot_general x2, matrix products, attention_block_fn(): jnp.einsum('bqc,ce->bqe', gated, out_weight, preferred_element_type=jnp.f...  2.27 us

profile of v1, /device:TPU:0, one launch (start us, length us, event | category | flops | bytes accessed | tf_op | source)
XLA Modules:
  0.0 102.5 jit_solution(10808646492546525615)
XLA Ops:
  0.7 0.7 add_multiply_fusion
  1.4 1.0 copy.50
  2.5 0.8 fusion.13
  3.4 0.6 copy.52
  4.0 13.1 %shard_map.149 = bf16[32,32,128]{2,1,0:T(8,128)(2,1)} custom-call(bf16[32,128]{1,0:T(8,128)(2,1)} %bitcast.156), custom_call_target="tpu_custom_call" | custom-call | tf_op jit(solution)/shard_map/pallas_call | solution.py:50
  17.1 1.0 copy.53
  18.2 0.2 copy.54
  18.4 0.3 fusion.82
  19.0 0.4 fusion.83
  19.5 0.8 copy.47
  20.4 0.6 copy-done.2
  21.1 0.5 fusion.84
  21.6 1.3 %convolution_add_fusion = f32[2,8,128,128]{2,3,1,0:T(8,128)S(1)} fusion(bf16[2,128,8,32]{1,3,2,0:T(8,128)(2,1)} %bitcast.144, bf16[2,128,8,32]{1,3,2,0:T(8,128)(2,1)} %bitcast.142, f32[8,128,128]{1,2,0:T(8,128)S(1)} %copy.54), kind=kOutput, calls=%fused_computation.9 | convolution fusion | flops 17039360 | bytes 1835008 | tf_op jit(solution)/shard_map/bqhd,bkhd->bhqk/dot_general | solution.py:95
  22.9 1.2 %fusion.19 = f32[2,8,32,128]{3,2,1,0:T(8,128)S(1)} fusion(bf16[2,128,8,32]{1,3,2,0:T(8,128)(2,1)} %bitcast.155, f32[2,8,128]{2,1,0:T(8,128)S(1)} %fusion.84, f32[2,8,128,128]{2,3,1,0:T(8,128)S(1)} %convolution_add_fusion), kind=kOutput, calls=%fused_computation.33 | convolution fusion | flops 17565824 | bytes 1449984 | tf_op jit(solution)/shard_map/bhqk,bkhd->bqhd/dot_general | solution.py:101
  24.3 1.1 %fusion.11 = bf16[2,128,256]{2,1,0:T(8,128)(2,1)S(1)} fusion(f32[2,128,256]{2,1,0:T(8,128)S(1)} %get-tuple-element.15, f32[2,128,256]{2,1,0:T(8,128)S(1)} %copy.56, f32[2,128,1024]{2,1,0:T(8,128)S(1)} %get-tuple-element.17, bf16[256,256]{1,0:T(8,128)(2,1)} %param.21), kind=kOutput, calls=%fused_computation.19 | convolution fusion | flops 34013184 | bytes 1048576 | tf_op jit(solution)/shard_map/bqc,ce->bqe/dot_general | solution.py:103
  25.5 0.7 reshape.173.source
  26.3 10.9 %shard_map.150 = bf16[32,4,512]{2,1,0:T(4,128)(2,1)} custom-call(bf16[32,4,512]{2,1,0:T(4,128)(2,1)} %reshape.173.source), custom_call_target="tpu_custom_call" | custom-call | tf_op jit(solution)/shard_map/pallas_call | solution.py:50
  37.2 1.0 reshape.188
  38.5 0.3 fusion.85
  39.3 0.5 fusion.86
  39.8 0.8 copy.59
  40.6 0.3 fusion.88
  41.0 1.3 %fusion.18 = f32[4,8,32,64]{3,2,1,0:T(8,128)S(1)} fusion(bf16[4,64,8,32]{1,3,2,0:T(8,128)(2,1)} %bitcast.153, f32[4,8,64]{2,1,0:T(8,128)S(1)} %fusion.86, f32[4,8,64,64]{2,3,1,0:T(8,128)S(1)} %fusion.88), kind=kOutput, calls=%fused_computation.32 | convolution fusion | flops 8783935 | bytes 925696 | tf_op jit(solution)/shard_map/bhqk,bkhd->bqhd/dot_general | solution.py:101
  42.5 1.1 %fusion.43 = (bf16[64,4,256]{2,0,1:T(8,128)(2,1)S(1)}, f32[4,64,256]{2,1,0:T(8,128)S(1)}) fusion(f32[64,4,256]{2,1,0:T(4,128)S(1)} %reshape.188, bf16[256,256]{1,0:T(8,128)(2,1)} %param.23, f32[4,64,256]{2,1,0:T(8,128)S(1)} %copy.63, f32[4,64,1024]{2,1,0:T(8,128)S(1)} %get-tuple-element.19), kind=kOutput, calls=%fused_computation.69 | convolution fusion | flops 34013184 | bytes 1310720 | tf_op jit(solution)/shard_map/bqc,ce->bqe/dot_general | solution.py:103
  43.6 0.8 copy.81
  44.5 0.2 multiply_reduce_fusion.2
  44.7 0.3 convolution_convert_fusion.1
  45.0 0.6 copy-done.4
  45.7 0.7 reshape_reshape.3.source
  46.4 16.3 %shard_map.151 = bf16[32,64,128]{2,1,0:T(8,128)(2,1)} custom-call(bf16[64,128]{1,0:T(8,128)(2,1)} %reshape_reshape.3.source), custom_call_target="tpu_custom_call" | custom-call | tf_op jit(solution)/shard_map/pallas_call | solution.py:50
  62.7 2.7 %reshape.178 = bf16[128,64,32]{2,1,0:T(8,128)(2,1)S(1)} reshape(bf16[32,64,128]{2,1,0:T(8,128)(2,1)} %shard_map.151) | data formatting | bytes 1048576 | tf_op jit(solution)/shard_map/reshape | solution.py:184
  65.4 2.6 %copy.86 = bf16[128,64,32,1]{0,1,3,2:T(8,128)(2,1)S(1)} copy(bf16[128,64,32,1]{2,1,0,3:T(8,128)(2,1)S(1)} %bitcast.130) | data formatting | bytes 1048576 | tf_op jit(solution)/shard_map/reshape | solution.py:184
  68.1 0.4 fusion.6
  68.5 0.7 copy.67
  69.2 0.4 fusion.87
  69.6 0.3 fusion.10
  69.9 0.3 convolution_bitcast_fusion
  70.8 0.9 copy.75
  71.7 14.2 %shard_map.152 = bf16[32,32,128]{2,1,0:T(8,128)(2,1)} custom-call(bf16[32,32,128]{2,1,0:T(8,128)(2,1)} %bitcast.136), custom_call_target="tpu_custom_call" | custom-call | tf_op jit(solution)/shard_map/pallas_call | solution.py:50
  85.9 1.1 %fusion.81 = (bf16[1,4,32,4,128]{4,3,1,0,2:T(4,128)(2,1)S(1)}, bf16[1,4,32,4,128]{4,3,1,0,2:T(4,128)(2,1)S(1)}) fusion(bf16[2,4,32,4,128]{4,3,1,0,2:T(4,128)(2,1)} %bitcast.135), kind=kLoop, calls=%fused_computation.133 | loop fusion | bytes 524288 | tf_op jit(solution)/shard_map/slice | solution.py:224
  87.1 0.2 convolution_convert_fusion
  87.3 0.7 copy.78
  88.0 10.9 %shard_map.153 = bf16[32,16,128]{2,1,0:T(8,128)(2,1)} custom-call(bf16[32,16,128]{2,1,0:T(8,128)(2,1)} %bitcast.150), custom_call_target="tpu_custom_call" | custom-call | tf_op jit(solution)/shard_map/pallas_call | solution.py:50
  98.9 1.1 %convert_reduce_fusion.1 = f32[4,128]{1,0:T(4,128)S(1)} fusion(bf16[128,4,128]{2,1,0:T(4,128)(2,1)} %bitcast.132), kind=kLoop, calls=%fused_computation.103 | loop fusion | flops 130560 | bytes 133120 | tf_op jit(solution)/shard_map/reduce_sum | solution.py:63
  100.0 1.0 %copy.79 = f32[128,4,128]{0,2,1:T(8,128)S(1)} copy(bf16[128,4,128]{2,1,0:T(4,128)(2,1)} %bitcast.133) | data formatting | bytes 393216 | tf_op jit(solution)/shard_map/convert_element_type | solution.py:231
  101.0 0.2 multiply_reduce_fusion
  101.3 0.4 fusion.12
  101.7 0.8 copy.82
  (64 shorter events, 2.7 us)
Async XLA Ops:
  0.6 18.3 %copy-start = (bf16[256,1024]{1,0:T(8,128)(2,1)S(1)}, bf16[256,1024]{1,0:T(8,128)(2,1)}, u32[]{:S(2)}) copy-start(bf16[256,1024]{1,0:T(8,128)(2,1)} %param.20) | copy-start | bytes 1572868
  0.6 17.8 %copy-start.11 = (bf16[23,256]{1,0:T(8,128)(2,1)S(1)}, bf16[23,256]{1,0:T(8,128)(2,1)}, u32[]{:S(2)}) copy-start(bf16[23,256]{1,0:T(8,128)(2,1)} %param.18) | copy-start | bytes 35332
  0.7 17.8 %copy-start.7 = (bf16[2,128,256]{2,1,0:T(8,128)(2,1)S(1)}, bf16[2,128,256]{2,1,0:T(8,128)(2,1)}, u32[]{:S(2)}) copy-start(bf16[2,128,256]{2,1,0:T(8,128)(2,1)} %param.16) | copy-start | bytes 393220
  0.7 17.8 %copy-start.12 = (s32[2,128]{1,0:T(2,128)S(1)}, s32[2,128]{1,0:T(2,128)}, u32[]{:S(2)}) copy-start(s32[2,128]{1,0:T(2,128)} %param.14) | copy-start | bytes 3076
  19.5 0.9 copy-start.1
  20.4 0.7 copy-start.2
  24.1 14.4 %copy-start.3 = (bf16[256,1024]{1,0:T(8,128)(2,1)S(1)}, bf16[256,1024]{1,0:T(8,128)(2,1)}, u32[]{:S(2)}) copy-start(bf16[256,1024]{1,0:T(8,128)(2,1)} %param.22) | copy-start | bytes 1572868
  42.3 2.4 %copy-start.9 = (bf16[256,64]{0,1:T(8,128)(2,1)S(1)}, bf16[256,64]{0,1:T(8,128)(2,1)}, u32[]{:S(2)}) copy-start(bf16[256,64]{0,1:T(8,128)(2,1)} %param.24) | copy-start | bytes 98308
  45.0 0.6 copy-start.4
  62.7 5.3 %copy-start.5 = (bf16[4,64,64]{1,2,0:T(8,128)(2,1)S(1)}, bf16[4,64,64]{1,2,0:T(8,128)(2,1)}, u32[]{:S(2)}) copy-start(bf16[4,64,64]{1,2,0:T(8,128)(2,1)} %copy-done.4) | copy-start | bytes 98308
  68.0 1.1 %copy-start.6 = (bf16[1024,128]{1,0:T(8,128)(2,1)S(1)}, bf16[1024,128]{1,0:T(8,128)(2,1)}, u32[]{:S(2)}) copy-start(bf16[1024,128]{1,0:T(8,128)(2,1)} %param.25) | copy-start | bytes 786436
  68.5 1.2 %copy-start.8 = (bf16[128,640]{1,0:T(8,128)(2,1)S(1)}, bf16[128,640]{1,0:T(8,128)(2,1)}, u32[]{:S(2)}) copy-start(bf16[128,640]{1,0:T(8,128)(2,1)} %param.26) | copy-start | bytes 491524
  70.7 30.6 %copy-start.10 = (bf16[128,128]{1,0:T(8,128)(2,1)S(1)}, bf16[128,128]{1,0:T(8,128)(2,1)}, u32[]{:S(2)}) copy-start(bf16[128,128]{1,0:T(8,128)(2,1)} %param.27) | copy-start | bytes 98308

commit v2 on v0

v2 whole, which is shorter than its diff:
```python
import functools

import jax
import jax.numpy as jnp
from jax import lax
from jax.experimental import pallas as pl
from jax.experimental.pallas import tpu as pltpu
from jax.sharding import PartitionSpec as P

EPSILON = 1e-05
MESH = pl.DeviceIdType.MESH
F32 = jnp.float32
BF16 = jnp.bfloat16
LANES = 128
SUBLANES = 8


def normalized(rows, axis=-1):
    average = jnp.mean(rows, axis, keepdims=True)
    centred = rows - average
    spread = jnp.mean(centred * centred, axis, keepdims=True)
    return (centred * lax.rsqrt(spread + EPSILON)).astype(BF16)


def product(lhs, rhs, lhs_axis=1, rhs_axis=0):
    return lax.dot_general(
        lhs, rhs, (((lhs_axis,), (rhs_axis,)), ((), ())), preferred_element_type=F32
    )


def permutation(size, major, minor):
    shift = minor.bit_length() - 1
    out = lax.broadcasted_iota(jnp.int32, (size, size), 0)
    came = lax.broadcasted_iota(jnp.int32, (size, size), 1)
    wanted = (out & (minor - 1)) * major + (out >> shift)
    return jnp.where(wanted == came, 1.0, 0.0).astype(BF16)


def swap_halves(first, second):
    half = SUBLANES // 2
    shape = first.shape
    first = first.reshape(-1, SUBLANES, shape[-1])
    second = second.reshape(-1, SUBLANES, shape[-1])
    upper = lax.broadcasted_iota(jnp.int32, first.shape, 1) < half
    low = jnp.where(upper, first, pltpu.roll(second, half, 1))
    high = jnp.where(upper, pltpu.roll(first, half, 1), second)
    return low.reshape(shape), high.reshape(shape)


def strided(wide, first, rows, stride):
    return jnp.concatenate(
        [wide[t, pl.ds(first, rows, stride=stride), :] for t in range(wide.shape[0])], 1
    )


def spread_tiles(wide, rows):
    for t in range(wide.shape[0]):
        wide[t] = rows[:, t * LANES : (t + 1) * LANES]


def attention(projected, channels, head_size, extra):
    rows = projected.shape[0]
    per_tile = LANES // head_size
    owner = lax.broadcasted_iota(jnp.int32, (rows, LANES), 1) >> (head_size.bit_length() - 1)
    pieces = []
    for tile in range(channels // LANES):
        part = lambda block: projected[:, block * channels + tile * LANES :][:, :LANES]
        query = part(0) * head_size ** (-0.5)
        key = part(1).astype(BF16)
        value = part(2)
        queries = jnp.concatenate(
            [jnp.where(owner == t, query, 0.0).astype(BF16) for t in range(per_tile)], 0
        )
        values = jnp.concatenate(
            [jnp.where(owner == t, value, 0.0).astype(BF16) for t in range(per_tile)], 0
        )
        scores = product(queries, key, 1, 1) + jnp.concatenate(
            [extra(tile * per_tile + t) for t in range(per_tile)], 0
        )
        top = jnp.max(scores, -1, keepdims=True)
        raised = jnp.exp(scores - top)
        weights = (raised * (1.0 / jnp.sum(raised, -1, keepdims=True))).astype(BF16)
        weights = jnp.concatenate(
            [weights[t * rows : (t + 1) * rows] for t in range(per_tile)], 1
        )
        mixed = product(weights, values)
        pieces.append((jax.nn.sigmoid(part(3)) * mixed).astype(BF16))
    return jnp.concatenate(pieces, 1)


def block_kernel(
    count,
    ids,
    mask,
    state,
    pair,
    lookup,
    bias_weight,
    row_weight,
    row_readout,
    column_weight,
    column_readout,
    factor_weight,
    outer_weight,
    tri_weight,
    tri_out_weight,
    msa_out,
    pair_out,
    bias_land,
    bias_wide,
    msa_send,
    msa_land,
    right_land,
    outer_wide,
    folded,
    tri_wide,
    tri_send,
    tri_land,
    back_send,
    back_land,
    back_wide,
    send_sems,
    recv_sems,
):
    me = lax.axis_index("res")
    seqs, chain, channels = state.shape
    owned, _, pair_chan = pair.shape
    heads = bias_weight.shape[1]
    head_size = channels // heads
    total = seqs * count
    classes = lookup.shape[0]
    width = factor_weight.shape[1] // 2
    held = pair_chan // count

    barrier = pltpu.get_barrier_semaphore()

    @pl.loop(1, count)
    def _(step):
        pl.semaphore_signal(
            barrier,
            inc=1,
            device_id={"res": lax.rem(me + step, count)},
            device_id_type=MESH,
        )

    def send(phase, landing, outgoing=None):
        @pl.loop(1, count)
        def _(step):
            peer = lax.rem(me + step, count)
            pltpu.make_async_remote_copy(
                src_ref=landing.at[me] if outgoing is None else outgoing.at[peer],
                dst_ref=landing.at[me],
                send_sem=send_sems.at[phase],
                recv_sem=recv_sems.at[phase],
                device_id={"res": peer},
                device_id_type=MESH,
            ).start()

    def drain(sems, phase, landing):
        others = landing.at[pl.ds(0, count - 1)]
        pltpu.make_async_copy(others, others, sems.at[phase]).wait()

    pair_rows = pair[...].astype(F32).reshape(owned * chain, pair_chan)
    bias = product(bias_weight[...], normalized(pair_rows), 0, 1)
    bias_land[me] = jnp.concatenate(
        [bias[:, i * chain : (i + 1) * chain] for i in range(owned)], 0
    ).astype(BF16)
    pl.semaphore_wait(barrier, count - 1)
    send(0, bias_land)

    starts = []
    for s in range(seqs):
        symbols = lax.broadcasted_iota(jnp.int32, (classes, chain), 0)
        hot = jnp.where(symbols == ids[s : s + 1, :], 1.0, 0.0).astype(BF16)
        starts.append(state[s].astype(F32) + product(hot, lookup[...], 0, 0))
    start = jnp.concatenate(starts, 0)
    projected = product(normalized(start), row_weight[...])
    masked = (mask[...].astype(F32) - 1.0) * 10000.0
    drain(recv_sems, 0, bias_land)
    spread_tiles(bias_wide, bias_land[...].astype(F32).reshape(-1, chain) + masked)
    extra = lambda head: strided(bias_wide, head, chain, heads)
    gated = jnp.concatenate(
        [
            attention(projected[s * chain : (s + 1) * chain], channels, head_size, extra)
            for s in range(seqs)
        ],
        0,
    )
    after_rows = (start + product(gated, row_readout[...])).astype(BF16)

    size = seqs * chain
    out = lax.broadcasted_iota(jnp.int32, (size, size), 0)
    came = lax.broadcasted_iota(jnp.int32, (size, size), 1)
    low_bits, seq_bits = owned.bit_length() - 1, seqs.bit_length() - 1
    wanted = (
        ((out >> low_bits) & (seqs - 1)) * chain
        + (out >> (low_bits + seq_bits)) * owned
        + (out & (owned - 1))
    )
    order = jnp.where(wanted == came, 1.0, 0.0).astype(BF16)
    moved = product(order, after_rows)
    group = seqs * owned
    msa_send[...] = jnp.concatenate(
        [
            moved[:, t * LANES : (t + 1) * LANES].reshape(count, group, LANES)
            for t in range(channels // LANES)
        ],
        1,
    ).astype(BF16)
    msa_land[me] = msa_send[me]
    send(1, msa_land, msa_send)
    outer_wide[...] = outer_weight[...].astype(F32)
    by_residue = permutation(total * owned, owned, total)
    by_sequence = permutation(total * owned, total, owned)
    drain(recv_sems, 1, msa_land)

    arrived = msa_land[...].astype(F32)
    arrived = jnp.concatenate(
        [
            arrived[:, t * group : (t + 1) * group].reshape(total * owned, LANES)
            for t in range(channels // LANES)
        ],
        1,
    ).astype(BF16)
    columns = product(by_residue, arrived)
    projected = product(normalized(columns), column_weight[...])
    joined = max(total, LANES)
    bits = total.bit_length() - 1
    same = (lax.broadcasted_iota(jnp.int32, (joined, joined), 0) >> bits) == (
        lax.broadcasted_iota(jnp.int32, (joined, joined), 1) >> bits
    )
    apart = jnp.where(same, 0.0, -1e30)
    gated = jnp.concatenate(
        [
            attention(projected[g : g + joined], channels, head_size, lambda head: apart)
            for g in range(0, total * owned, joined)
        ],
        0,
    )
    after = columns + product(gated, column_readout[...])

    outer_in = normalized(after)
    left = product(outer_in, factor_weight[...])[:, :width].astype(BF16)
    right = product(factor_weight[...], outer_in, 0, 1)[width:]
    packed = LANES // total
    slots = width // packed
    right = jnp.concatenate(
        [
            jnp.concatenate(
                [
                    right[p * slots : (p + 1) * slots, r * total : (r + 1) * total]
                    for p in range(packed)
                ],
                1,
            )
            for r in range(owned)
        ],
        0,
    ).astype(BF16)
    right_land[me] = product(permutation(slots * owned, slots, owned), right).astype(BF16)
    send(2, right_land)
    msa_out[...] = product(by_sequence, after.astype(BF16)).astype(BF16)
    for k in range(width):
        slot, p = k // packed, k % packed
        weight = outer_wide[pl.ds(p * slots + slot, width, stride=width), :].astype(BF16)
        part = product(left, weight).astype(BF16)
        for i in range(owned):
            folded[k * total : (k + 1) * total, i * pair_chan : (i + 1) * pair_chan] = part[
                i * total : (i + 1) * total
            ]
    drain(recv_sems, 2, right_land)
    wide = right_land[...].astype(F32)
    tiles = slots * owned // SUBLANES
    wide = wide.reshape(count // 2, 2, tiles, SUBLANES, LANES)
    low, high = swap_halves(wide[:, 0], wide[:, 1])
    right_rows = jnp.concatenate(
        [
            half[:, t].reshape(chain, LANES).astype(BF16)
            for t in range(tiles)
            for half in (low, high)
        ],
        1,
    )
    update = product(right_rows, folded[...]) * (1.0 / total)
    pair_one = pair_rows + jnp.concatenate(
        [update[:, i * pair_chan : (i + 1) * pair_chan] for i in range(owned)], 0
    )

    tri_in = normalized(pair_one)
    factors = product(tri_weight[:, : 4 * pair_chan], tri_in, 0, 1)
    for side in range(2):
        plain = factors[2 * side * pair_chan : (2 * side + 1) * pair_chan]
        gate = factors[(2 * side + 1) * pair_chan : (2 * side + 2) * pair_chan]
        factor = jax.nn.sigmoid(gate) * plain
        for i in range(owned):
            for t in range(chain // LANES):
                tri_wide[t, pl.ds(side * owned + i, pair_chan, stride=2 * owned), :] = factor[
                    :, i * chain + t * LANES :
                ][:, :LANES]
    tri_send[...] = (
        jnp.concatenate([tri_wide[t] for t in range(chain // LANES)], 1)
        .astype(BF16)
        .reshape(tri_send.shape)
    )
    tri_land[me] = tri_send[me]
    send(3, tri_land, tri_send)
    gate_out = jax.nn.sigmoid(product(tri_in, tri_weight[:, 4 * pair_chan :]))
    drain(recv_sems, 3, tri_land)
    wide = tri_land[...].astype(F32).reshape(count // 2, 2, held, SUBLANES, chain)
    low, high = swap_halves(wide[:, 0], wide[:, 1])
    combined = [
        product(
            low[:, c].reshape(chain, chain).astype(BF16),
            high[:, c].reshape(chain, chain).astype(BF16),
            1,
            1,
        ).reshape(count // 2, SUBLANES, chain)
        for c in range(held)
    ]
    swapped = [swap_halves(combined[c], combined[c + 1]) for c in range(0, held, 2)]
    even = jnp.concatenate([low for low, _ in swapped], 1)
    odd = jnp.concatenate([high for _, high in swapped], 1)
    back_send[...] = (
        jnp.concatenate([even[:, None], odd[:, None]], 1)
        .reshape(back_send.shape)
        .astype(BF16)
    )
    back_land[me] = back_send[me]
    send(4, back_land, back_send)
    drain(recv_sems, 4, back_land)
    spread_tiles(back_wide, back_land[...].astype(F32).reshape(-1, chain))
    for i in range(owned):
        rows = slice(i * chain, (i + 1) * chain)
        mixed = normalized(strided(back_wide, i, pair_chan, owned), 0)
        tri_update = product(mixed, tri_out_weight[...], 0, 0)
        pair_out[i] = (pair_one[rows] + gate_out[rows] * tri_update).astype(BF16)

    for phase, landing in enumerate((bias_land, msa_land, right_land, tri_land, back_land)):
        drain(send_sems, phase, landing)


def shards(*operands):
    operands = list(operands)
    count = lax.axis_size("res")
    operands[1] = operands[1].reshape(1, -1)
    seqs, chain, channels = operands[2].shape
    owned, _, pair_chan = operands[3].shape
    heads = operands[5].shape[1]
    width = operands[10].shape[1] // 2
    total = seqs * count
    held = pair_chan // count
    vmem = pltpu.VMEM
    group = seqs * owned * channels // LANES
    factor_rows = width * total // LANES * owned
    msa, pair = pl.pallas_call(
        functools.partial(block_kernel, count),
        out_shape=(
            jax.ShapeDtypeStruct((total * owned, channels), BF16),
            jax.ShapeDtypeStruct((owned, chain, pair_chan), BF16),
        ),
        in_specs=[pl.BlockSpec(memory_space=vmem)] * len(operands),
        out_specs=(pl.BlockSpec(memory_space=vmem),) * 2,
        scratch_shapes=[
            vmem((count, owned * heads, chain), BF16),
            vmem((chain // LANES, count * owned * heads, LANES), F32),
            vmem((count, group, LANES), BF16),
            vmem((count, group, LANES), BF16),
            vmem((count, factor_rows, LANES), BF16),
            vmem((width * width, pair_chan), F32),
            vmem((width * total, owned * pair_chan), BF16),
            vmem((chain // LANES, pair_chan * 2 * owned, LANES), F32),
            vmem((count, held * 2 * owned, chain), BF16),
            vmem((count, held * 2 * owned, chain), BF16),
            vmem((count, held * owned, chain), BF16),
            vmem((count, held * owned, chain), BF16),
            vmem((chain // LANES, pair_chan * owned, LANES), F32),
            pltpu.SemaphoreType.DMA((5,)),
            pltpu.SemaphoreType.DMA((5,)),
        ],
        compiler_params=pltpu.CompilerParams(
            collective_id=0, has_side_effects=True, vmem_limit_bytes=60 << 20
        ),
    )(*operands)
    return msa.reshape(total, owned, channels), pair


def solution(mesh):
    placed = (
        P(("crop", "res"), None),
        P("crop"),
        P(("crop", "res"), None, None),
        P(("crop", "res"), None, None),
    ) + (P(),) * 10
    return jax.shard_map(
        shards,
        mesh=mesh,
        in_specs=placed,
        out_specs=(P("crop", "res", None), P(("crop", "res"), None, None)),
        check_vma=False,
    )
```

time: 156 us -> 59.2 us (0.38)
  blocking collectives: 93.2 us -> 0 us
  Pallas kernels: 0 us -> 53.9 us
  waiting for transfers between devices: 22.7 us -> 0 us
  local copies, waits for them, and re-layouts: 17.4 us -> 4.43 us
  matrix products: 11 us -> 0 us
  starting transfers between devices: 7.73 us -> 0 us
  other arithmetic: 2.2 us -> 0 us
    all_gather x2 -> x0, blocking collectives: 83.3 us -> none  [the longest x1 43.9 us: shards(): bias_all = lax.all_gather(bias_local, 'res', axis=1, tiled=True)]
    pallas_call x0 -> x1, Pallas kernels: none -> 53.9 us  [shards(): pl.pallas_call(functools.partial(block_kernel, count), out_shape=(jax.Sha...]
    all_to_all x3 -> x0, waiting for transfers between devices: 22.7 us -> none  [the longest x1 8.14 us: shards(): lax.all_to_all(left_f, 'res', split_axis=0, concat_axis=2, tiled=True)]
    dot_general x17 -> x0, matrix products: 10 us -> none  [the longest x2 2.23 us: attention_block_fn(): jnp.einsum('bqc,ce->bqe', gated, out_weight, preferred_element_type=jnp.f...]
    all_to_all x1 -> x0, blocking collectives: 9.91 us -> none  [shards(): lax.all_to_all(alignment_after_rows, 'res', split_axis=1, concat_axis=0,...]
    all_to_all x3 -> x0, starting transfers between devices: 7.73 us -> none  [the longest x1 2.58 us: shards(): lax.all_to_all(left_f, 'res', split_axis=0, concat_axis=2, tiled=True)]
    reshape x6 -> x1, local copies, waits for them, and re-layouts: 7.55 us -> 1.63 us  [shards(): return (msa.reshape(total, owned, channels), pair)]
    slice x8 -> x0, local copies, waits for them, and re-layouts: 3.84 us -> none  [the longest x2 2.1 us: split_proj(): projected[..., 2 * channels:3 * channels].astype(jnp.bfloat16)]
  transfers between devices with their start and end apart: 3 -> 0, of which waited for: 3 -> 0; matrix products, arithmetic and copies ran while one was open for 1% -> 0% of each run, Pallas kernels for 0% -> 0%
where the time goes in v2:
time: 59.2 us; the launch traced here: 59 us
  Pallas kernels  53.9 us (91%)
  local copies, waits for them, and re-layouts  4.43 us (7%)
  between operations  0.66 us (1%)
    pallas_call x1, Pallas kernels, shards(): pl.pallas_call(functools.partial(block_kernel, count), out_shape=(jax.Sha...  53.9 us
    unnamed x7, local copies, waits for them, and re-layouts  2.8 us
    reshape x1, local copies, waits for them, and re-layouts, shards(): return (msa.reshape(total, owned, channels), pair)  1.63 us

profile of v2, /device:TPU:0, one launch (start us, length us, event | category | flops | bytes accessed | tf_op | source)
XLA Modules:
  0.0 59.0 jit_solution(11674696988784062914)
XLA Ops:
  0.6 0.0 copy-start.1
  0.6 1.4 %copy.16.bias_weight = bf16[128,8]{1,0:T(8,128)(2,1)} copy(bf16[128,8]{0,1:T(8,128)(2,1)} %param.19) | data formatting | bytes 4096 | tf_op args[5]
  2.0 0.0 copy-done.1
  2.0 0.7 %copy.17.factor_weight = bf16[256,64]{1,0:T(8,128)(2,1)} copy(bf16[256,64]{0,1:T(8,128)(2,1)S(1)} %copy-done.1) | data formatting | bytes 65536 | tf_op args[10]
  2.8 53.9 %shard_map.149 = (bf16[256,256]{1,0:T(8,128)(2,1)}, bf16[4,128,128]{2,1,0:T(8,128)(2,1)}) custom-call(s32[2,128]{1,0:T(2,128)} %ids.1, s32[1,128]{1,0:T(1,128)} %bitcast.1, bf16[2,128,256]{2,1,0:T(8,128)(2,1)} %state.1, bf16[4,128,128]{2,1,0:T(8,128)(2,1)} %pair.1, bf16[23,256]{1,0:T(8,128)(2,1)} %lookup.1, bf16[128,8]{1,0:T(8,128)(2,1)} %copy.16.bias_weight, ...), custom_call_target="tpu_custom_call" | custom-call | tf_op jit(solution)/shard_map/pallas_call | solution.py:355
  56.7 0.0 copy-start
  56.7 1.6 %reshape.11 = bf16[64,4,256]{2,1,0:T(4,128)(2,1)} reshape(bf16[256,256]{1,0:T(8,128)(2,1)} %get-tuple-element.4) | data formatting | bytes 262144 | tf_op jit(solution)/shard_map/reshape | solution.py:384
  58.3 0.0 copy-done
  58.3 0.7 %copy.19 = bf16[4,128,128]{2,1,0:T(8,128)(2,1)} copy(bf16[4,128,128]{2,1,0:T(8,128)(2,1)S(1)} %copy-done) | data formatting | bytes 262144
Async XLA Ops:
  0.6 1.4 %copy-start.1 = (bf16[256,64]{0,1:T(8,128)(2,1)S(1)}, bf16[256,64]{0,1:T(8,128)(2,1)}, u32[]{:S(2)}) copy-start(bf16[256,64]{0,1:T(8,128)(2,1)} %param.24) | copy-start | bytes 98308
  56.7 1.6 %copy-start = (bf16[4,128,128]{2,1,0:T(8,128)(2,1)S(1)}, bf16[4,128,128]{2,1,0:T(8,128)(2,1)}, u32[]{:S(2)}) copy-start(bf16[4,128,128]{2,1,0:T(8,128)(2,1)} %get-tuple-element.9) | copy-start | bytes 393220

commit v3 on v2

--- a/solution.py
+++ b/solution.py
@@ -125,11 +125,11 @@
     me = lax.axis_index("res")
     seqs, chain, channels = state.shape
     owned, _, pair_chan = pair.shape
-    heads = bias_weight.shape[1]
+    heads = bias_weight.shape[0]
     head_size = channels // heads
     total = seqs * count
     classes = lookup.shape[0]
-    width = factor_weight.shape[1] // 2
+    width = factor_weight.shape[0] // 2
     held = pair_chan // count
 
     barrier = pltpu.get_barrier_semaphore()
@@ -139,14 +139,14 @@
         pl.semaphore_signal(
             barrier,
             inc=1,
-            device_id={"res": lax.rem(me + step, count)},
+            device_id={"res": me ^ (count - step)},
             device_id_type=MESH,
         )
 
     def send(phase, landing, outgoing=None):
         @pl.loop(1, count)
         def _(step):
-            peer = lax.rem(me + step, count)
+            peer = me ^ (count - step)
             pltpu.make_async_remote_copy(
                 src_ref=landing.at[me] if outgoing is None else outgoing.at[peer],
                 dst_ref=landing.at[me],
@@ -161,7 +161,7 @@
         pltpu.make_async_copy(others, others, sems.at[phase]).wait()
 
     pair_rows = pair[...].astype(F32).reshape(owned * chain, pair_chan)
-    bias = product(bias_weight[...], normalized(pair_rows), 0, 1)
+    bias = product(bias_weight[...], normalized(pair_rows), 1, 1)
     bias_land[me] = jnp.concatenate(
         [bias[:, i * chain : (i + 1) * chain] for i in range(owned)], 0
     ).astype(BF16)
@@ -240,8 +240,8 @@
     after = columns + product(gated, column_readout[...])
 
     outer_in = normalized(after)
-    left = product(outer_in, factor_weight[...])[:, :width].astype(BF16)
-    right = product(factor_weight[...], outer_in, 0, 1)[width:]
+    left = product(outer_in, factor_weight[:width, :], 1, 1).astype(BF16)
+    right = product(factor_weight[width:, :], outer_in, 1, 1)
     packed = LANES // total
     slots = width // packed
     right = jnp.concatenate(
@@ -259,7 +259,9 @@
     ).astype(BF16)
     right_land[me] = product(permutation(slots * owned, slots, owned), right).astype(BF16)
     send(2, right_land)
-    msa_out[...] = product(by_sequence, after.astype(BF16)).astype(BF16)
+    msa_out[...] = (
+        product(by_sequence, after.astype(BF16)).reshape(msa_out.shape).astype(BF16)
+    )
     for k in range(width):
         slot, p = k // packed, k % packed
         weight = outer_wide[pl.ds(p * slots + slot, width, stride=width), :].astype(BF16)
@@ -343,10 +345,12 @@
     operands = list(operands)
     count = lax.axis_size("res")
     operands[1] = operands[1].reshape(1, -1)
+    operands[5] = operands[5].T
+    operands[10] = operands[10].T
     seqs, chain, channels = operands[2].shape
     owned, _, pair_chan = operands[3].shape
-    heads = operands[5].shape[1]
-    width = operands[10].shape[1] // 2
+    heads = operands[5].shape[0]
+    width = operands[10].shape[0] // 2
     total = seqs * count
     held = pair_chan // count
     vmem = pltpu.VMEM
@@ -355,7 +359,7 @@
     msa, pair = pl.pallas_call(
         functools.partial(block_kernel, count),
         out_shape=(
-            jax.ShapeDtypeStruct((total * owned, channels), BF16),
+            jax.ShapeDtypeStruct((total, owned, channels), BF16),
             jax.ShapeDtypeStruct((owned, chain, pair_chan), BF16),
         ),
         in_specs=[pl.BlockSpec(memory_space=vmem)] * len(operands),
@@ -381,7 +385,7 @@
             collective_id=0, has_side_effects=True, vmem_limit_bytes=60 << 20
         ),
     )(*operands)
-    return msa.reshape(total, owned, channels), pair
+    return msa, pair
 
 
 def solution(mesh):

time: 59.2 us -> 54.4 us (0.919)
  Pallas kernels: 53.9 us -> 51.3 us
  local copies, waits for them, and re-layouts: 4.43 us -> 2.3 us
    pallas_call x1, Pallas kernels: 53.9 us -> 51.3 us  [shards(): pl.pallas_call(functools.partial(block_kernel, count), out_shape=(jax.Sha...]
    reshape x1 -> x0, local copies, waits for them, and re-layouts: 1.63 us -> none  [shards(): return (msa.reshape(total, owned, channels), pair)]
    unnamed x7 -> x4, local copies, waits for them, and re-layouts: 2.8 us -> 2.3 us
where the time goes in v3:
time: 54.4 us; the launch traced here: 54.2 us
  Pallas kernels  51.3 us (94%)
  local copies, waits for them, and re-layouts  2.3 us (4%)
  between operations  0.65 us (1%)
    pallas_call x1, Pallas kernels, shards(): pl.pallas_call(functools.partial(block_kernel, count), out_shape=(jax.Sha...  51.3 us
    unnamed x4, local copies, waits for them, and re-layouts  2.3 us

profile of v3, /device:TPU:0, one launch (start us, length us, event | category | flops | bytes accessed | tf_op | source)
XLA Modules:
  0.0 54.2 jit_solution(16812647724308472118)
XLA Ops:
  0.6 51.3 %shard_map.149 = (bf16[64,4,256]{2,1,0:T(4,128)(2,1)}, bf16[4,128,128]{2,1,0:T(8,128)(2,1)}) custom-call(s32[2,128]{1,0:T(2,128)} %ids.1, s32[1,128]{1,0:T(1,128)} %bitcast.5, bf16[2,128,256]{2,1,0:T(8,128)(2,1)} %state.1, bf16[4,128,128]{2,1,0:T(8,128)(2,1)} %pair.1, bf16[23,256]{1,0:T(8,128)(2,1)} %lookup.1, bf16[8,128]{1,0:T(8,128)(2,1)} %bitcast.4, ...), custom_call_target="tpu_custom_call" | custom-call | tf_op jit(solution)/shard_map/pallas_call | solution.py:359
  51.9 0.0 copy-start
  51.9 1.6 %copy.18 = bf16[64,4,256]{2,1,0:T(4,128)(2,1)} copy(bf16[64,4,256]{2,1,0:T(4,128)(2,1)} %get-tuple-element.4) | data formatting | bytes 262144
  53.6 0.0 copy-done
  53.6 0.7 %copy.19 = bf16[4,128,128]{2,1,0:T(8,128)(2,1)} copy(bf16[4,128,128]{2,1,0:T(8,128)(2,1)S(1)} %copy-done) | data formatting | bytes 262144
Async XLA Ops:
  51.9 1.7 %copy-start = (bf16[4,128,128]{2,1,0:T(8,128)(2,1)S(1)}, bf16[4,128,128]{2,1,0:T(8,128)(2,1)}, u32[]{:S(2)}) copy-start(bf16[4,128,128]{2,1,0:T(8,128)(2,1)} %get-tuple-element.5) | copy-start | bytes 393220
